TPU v7x, 32 devices: a whole 2x2x4 slice. The times are simulated.
32 devices in a mesh: freq: 2 (over y), rcv: 4 (over z), src: 4 (over x, core).
Axes of the slice: x: 2, y: 2, z: 4, core: 2. Of those that a mesh axis runs over, the one named last changes fastest.
Arguments:
- traces: float32 [256, 2, 4096], P(('freq', 'src'), None, 'rcv'), parts along dimension 0, may hold values from -6 to 6
- moveout: float32 [2, 64, 16], P(None, 'freq'), parts along dimension 1, may hold values from -0.75 to 0.75
- trace_owner: int32 [8192], P(('freq', 'rcv')), parts along dimension 0, may hold values from 0 to 3, as said below
- trace_group: int32 [8192], P(('freq', 'rcv')), parts along dimension 0, may hold values from 0 to 127
- trace_table: int32 [8192], P(('freq', 'rcv')), parts along dimension 0, may hold values from 0 to 31
- aperture: float32 [2, 16384, 8192], P(None, ('freq', 'rcv'), 'src'), parts along dimension 1, may hold values from -0.046875 to 0.046875
- shaping: float32 [256, 2, 8192], P(('freq', 'src'), None, 'rcv'), parts along dimension 0, may hold values from -0.5 to 0.5
Outputs:
- demultiple: float32 [256, 2, 8192], P(('freq', 'src'), None, 'rcv'), parts along dimension 0
There are 2 independent parts, one for each index of `freq`. A program takes and returns all parts, laid end to end along the dimension named above; each array names one. Nothing has to cross between parts.
Inputs may be any that keep to these rules, and one draw needn't show every extreme that they name: `trace_owner`: among the 1024 traces of each index of rcv (aligned blocks of the array), at most 512 name the same owner, and in every draw some owner is named by exactly 512 traces of every block.
All inputs are finite; a program needn't handle non-finite values.
Results may differ from a plain program's by a relative error of at most 0.0001.
Values sent between devices are 32-bit elements; how exact they have to be, the bound alone decides.
A program may use at most 128 MiB of HBM per device.

v0:
```python
import jax
import jax.numpy as jnp
from jax import lax
from jax.sharding import PartitionSpec as P

ITERS = 2


def from_root(value, axis, source):
    kept = jnp.where(lax.axis_index(axis) == source, value, 0).astype(value.dtype)
    return lax.psum(kept, axis)


def complex_join(partial_terms):
    return jnp.stack(
        [
            partial_terms[:, 0, 0] - partial_terms[:, 1, 1],
            partial_terms[:, 0, 1] + partial_terms[:, 1, 0],
        ],
        axis=1,
    )


def complex_product(left_side, right_side):
    real_part = left_side[:, 0] * right_side[:, 0] - left_side[:, 1] * right_side[:, 1]
    imag_part = left_side[:, 0] * right_side[:, 1] + left_side[:, 1] * right_side[:, 0]
    return jnp.stack([real_part, imag_part], axis=1)


def bin_matrix(group_code, table_code, moveout, groups, owner_mask):
    group_hot = (group_code[:, None] == jnp.arange(groups)[None, :]).astype(jnp.float32)
    group_hot = group_hot * owner_mask[:, None]
    table_hot = (table_code[:, None] == jnp.arange(moveout.shape[1])[None, :]).astype(jnp.float32)
    weights = jnp.einsum("tk,ckj->tcj", table_hot, moveout, precision=lax.Precision.HIGHEST)
    matrix = group_hot[:, None, :, None] * weights[:, :, None, :]
    return matrix.reshape(matrix.shape[0], 2, groups * moveout.shape[2])


def interpolate(values, matrix):
    return complex_join(
        jnp.einsum("sct,tdb->scdb", values, matrix, precision=lax.Precision.HIGHEST)
    )


def to_columns(panel_now):
    shots_all = lax.all_gather(panel_now, "src", axis=0, tiled=True)
    fold_count = lax.axis_size("rcv") // lax.axis_size("src")
    first_root = fold_count * lax.axis_index("src")
    pieces = [from_root(shots_all, "rcv", first_root + offset) for offset in range(fold_count)]
    return jnp.concatenate(pieces, axis=2)


def multiply(columns, aperture):
    return lax.psum_scatter(
        complex_join(
            jnp.einsum("sck,dik->scdi", columns, aperture, precision=lax.Precision.HIGHEST)
        ),
        "src",
        scatter_dimension=0,
        tiled=True,
    )


def per_device(traces, moveout, trace_owner, trace_group, trace_table, aperture, shaping):
    groups = aperture.shape[1] // moveout.shape[2]

    def one_owner(owner_index):
        owner_mask = (trace_owner == owner_index).astype(jnp.float32)
        matrix = bin_matrix(trace_group, trace_table, moveout, groups, owner_mask)
        return interpolate(traces, matrix)

    binned = lax.psum_scatter(
        lax.map(one_owner, jnp.arange(1 * lax.axis_size("rcv"), dtype=jnp.int32)),
        "rcv",
        scatter_dimension=0,
        tiled=True,
    )[0]
    panel_now = binned
    for sweep_index in range(ITERS):
        multiples = multiply(to_columns(panel_now), aperture)
        panel_now = binned - complex_product(shaping, multiples)
    return panel_now


def solution(mesh):
    in_specs = (
        P(("freq", "src"), None, "rcv"),
        P(None, "freq", None),
        P(("freq", "rcv")),
        P(("freq", "rcv")),
        P(("freq", "rcv")),
        P(None, ("freq", "rcv"), "src"),
        P(("freq", "src"), None, "rcv"),
    )
    out_specs = P(("freq", "src"), None, "rcv")
    return jax.shard_map(
        per_device, mesh=mesh, in_specs=in_specs, out_specs=out_specs, check_vma=False
    )
```

profile of v0, /device:TPU:0, one launch (start us, length us, event | category | flops | bytes accessed | tf_op | source)
XLA Modules:
  0.0 581.3 jit_solution(2520688945853668558)
XLA Ops:
  6.5 1.0 copy.18
  7.6 160.8 %while.10 = (s32[]{:T(128)}, f32[4,32,2,2048]{3,1,2,0:T(8,128)}, s32[1024]{0:T(1024)}, s32[4]{0:T(128)S(1)}, s32[1024]{0:T(1024)}, /*index=5*/s32[1024]{0:T(1024...) while((s32[]{:T(128)}, f32[4,32,2,2048]{3,1,2,0:T(8,128)}, s32[1024]{0:T(1024)}, s32[4]{0:T(128)S(1)}, ...), condition=%wide.region_1.2_spmd, body=%wide.region_0.1_spmd.sunk | while | flops 3238561792 | bytes 55632548 | solution.py:73
  7.6 0.6 dynamic_slice.5
  8.2 1.3 compare_convert_fusion.2
  9.5 0.7 fusion.38
  10.3 4.3 mul.92
  14.8 12.2 %bitcast_multiply_fusion.2 = f32[1024,2,2048]{0,2,1:T(8,128)} fusion(f32[1024,2,16]{0,2,1:T(8,128)S(1)} %bitcast.96, f32[1024,2048]{0,1:T(8,128)} %bitcast.95), kind=kLoop, calls=%fused_computation.2.clone.1 | loop fusion | flops 4194304 | bytes 25296896 | tf_op jit(solution)/shard_map/while/body/eval_jaxpr/mul | solution.py:35
  27.1 19.8 %fusion.39 = f32[32,2,2,2048]{3,0,1,2:T(8,128)S(1)} fusion(f32[1024,2,2048]{0,2,1:T(8,128)} %bitcast_multiply_fusion.2, f32[32,2,1024]{2,0,1:T(8,128)S(1)} %get-tuple-element.164), kind=kOutput, calls=%fused_computation.3.clone.1 | convolution fusion | flops 3221225472 | bytes 18087936 | tf_op jit(solution)/shard_map/while/body/eval_jaxpr/sct,tdb->scdb/dot_general | solution.py:41
  46.9 0.9 fusion.42
  47.8 0.6 dynamic_slice.5
  48.4 1.3 compare_convert_fusion.2
  49.7 0.7 fusion.38
  50.5 4.3 mul.92
  55.0 12.2 %bitcast_multiply_fusion.2 = f32[1024,2,2048]{0,2,1:T(8,128)} fusion(f32[1024,2,16]{0,2,1:T(8,128)S(1)} %bitcast.96, f32[1024,2048]{0,1:T(8,128)} %bitcast.95), kind=kLoop, calls=%fused_computation.2.clone.1 | loop fusion | flops 4194304 | bytes 25296896 | tf_op jit(solution)/shard_map/while/body/eval_jaxpr/mul | solution.py:35
  67.3 19.8 %fusion.39 = f32[32,2,2,2048]{3,0,1,2:T(8,128)S(1)} fusion(f32[1024,2,2048]{0,2,1:T(8,128)} %bitcast_multiply_fusion.2, f32[32,2,1024]{2,0,1:T(8,128)S(1)} %get-tuple-element.164), kind=kOutput, calls=%fused_computation.3.clone.1 | convolution fusion | flops 3221225472 | bytes 18087936 | tf_op jit(solution)/shard_map/while/body/eval_jaxpr/sct,tdb->scdb/dot_general | solution.py:41
  87.1 0.9 fusion.42
  88.0 0.6 dynamic_slice.5
  88.6 1.3 compare_convert_fusion.2
  89.9 0.7 fusion.38
  90.7 4.3 mul.92
  95.2 12.2 %bitcast_multiply_fusion.2 = f32[1024,2,2048]{0,2,1:T(8,128)} fusion(f32[1024,2,16]{0,2,1:T(8,128)S(1)} %bitcast.96, f32[1024,2048]{0,1:T(8,128)} %bitcast.95), kind=kLoop, calls=%fused_computation.2.clone.1 | loop fusion | flops 4194304 | bytes 25296896 | tf_op jit(solution)/shard_map/while/body/eval_jaxpr/mul | solution.py:35
  107.5 19.8 %fusion.39 = f32[32,2,2,2048]{3,0,1,2:T(8,128)S(1)} fusion(f32[1024,2,2048]{0,2,1:T(8,128)} %bitcast_multiply_fusion.2, f32[32,2,1024]{2,0,1:T(8,128)S(1)} %get-tuple-element.164), kind=kOutput, calls=%fused_computation.3.clone.1 | convolution fusion | flops 3221225472 | bytes 18087936 | tf_op jit(solution)/shard_map/while/body/eval_jaxpr/sct,tdb->scdb/dot_general | solution.py:41
  127.3 0.9 fusion.42
  128.2 0.6 dynamic_slice.5
  128.8 1.3 compare_convert_fusion.2
  130.1 0.7 fusion.38
  130.9 4.3 mul.92
  135.4 12.2 %bitcast_multiply_fusion.2 = f32[1024,2,2048]{0,2,1:T(8,128)} fusion(f32[1024,2,16]{0,2,1:T(8,128)S(1)} %bitcast.96, f32[1024,2048]{0,1:T(8,128)} %bitcast.95), kind=kLoop, calls=%fused_computation.2.clone.1 | loop fusion | flops 4194304 | bytes 25296896 | tf_op jit(solution)/shard_map/while/body/eval_jaxpr/mul | solution.py:35
  147.6 19.8 %fusion.39 = f32[32,2,2,2048]{3,0,1,2:T(8,128)S(1)} fusion(f32[1024,2,2048]{0,2,1:T(8,128)} %bitcast_multiply_fusion.2, f32[32,2,1024]{2,0,1:T(8,128)S(1)} %get-tuple-element.164), kind=kOutput, calls=%fused_computation.3.clone.1 | convolution fusion | flops 3221225472 | bytes 18087936 | tf_op jit(solution)/shard_map/while/body/eval_jaxpr/sct,tdb->scdb/dot_general | solution.py:41
  167.5 0.9 fusion.42
  168.5 46.5 %reduce-scatter.4.cloned.1.call-done = f32[1,32,2,2048]{3,1,2,0:T(8,128)} async-done(((f32[4,32,2,2048]{3,1,2,0:T(8,128)}), f32[1,32,2,2048]{3,1,2,0:T(8,128)}) %reduce-scatter.4.cloned.1.call-update) | async-done | bytes 524304 | tf_op jit(solution)/shard_map/reduce_scatter | solution.py:72
  215.0 23.3 %all-gather.6.cloned.1.call-done = f32[1,128,2,2048]{3,1,2,0:T(8,128)} async-done(((f32[1,32,2,2048]{3,1,2,0:T(8,128)}), f32[1,128,2,2048]{3,1,2,0:T(8,128)}) %all-gather.6.cloned.1.call-update) | async-done | bytes 2097168 | tf_op jit(solution)/shard_map/all_gather | solution.py:46
  238.3 3.1 select_bitcast_fusion
  241.7 85.9 %all-reduce.3.cloned.1.call-done = f32[128,2,2048]{2,0,1:T(8,128)} async-done(((f32[128,2,2048]{2,0,1:T(8,128)}), f32[128,2,2048]{2,0,1:T(8,128)}) %all-reduce.3.cloned.1.call-update) | async-done | bytes 2097168 | tf_op jit(solution)/shard_map/psum | solution.py:11
  327.6 33.0 %fusion.15 = f32[128,2,2,2048]{3,0,2,1:T(8,128)S(1)} fusion(f32[2,2048,2048]{2,1,0:T(8,128)} %param.14, f32[128,2,2048]{2,0,1:T(8,128)} %all-reduce.3.cloned.1.call-done), kind=kOutput, calls=%fused_computation.21 | convolution fusion | flops 25769803776 | bytes 39845888 | tf_op jit(solution)/shard_map/sck,dik->scdi/dot_general | solution.py:56
  360.9 1.5 pad_maximum_fusion
  362.4 1.0 copy-done.1
  363.8 28.9 %reduce-scatter.6.cloned.1.call-done = f32[32,2,2048]{2,0,1:T(8,128)} async-done(((f32[128,2,2048]{2,0,1:T(8,128)}), f32[32,2,2048]{2,0,1:T(8,128)}) %reduce-scatter.6.cloned.1.call-update) | async-done | bytes 524304 | tf_op jit(solution)/shard_map/reduce_scatter | solution.py:54
  392.7 1.2 multiply_subtract_fusion.1
  393.9 0.9 maximum_subtract_fusion
  394.9 22.7 %all-gather.4.cloned.1.call-done = f32[128,2,2048]{2,0,1:T(8,128)} async-done(((f32[32,2,2048]{2,0,1:T(8,128)}), f32[128,2,2048]{2,0,1:T(8,128)}) %all-gather.4.cloned.1.call-update) | async-done | bytes 2097168 | tf_op jit(solution)/shard_map/all_gather | solution.py:46
  417.6 3.1 broadcast_select_fusion
  421.0 85.9 %all-reduce.5.cloned.1.call-done = f32[128,2,2048]{2,0,1:T(8,128)} async-done(((f32[128,2,2048]{2,0,1:T(8,128)}), f32[128,2,2048]{2,0,1:T(8,128)}) %all-reduce.5.cloned.1.call-update) | async-done | bytes 2097168 | tf_op jit(solution)/shard_map/psum | solution.py:11
  506.9 33.0 %fusion.13 = f32[128,2,2,2048]{3,0,2,1:T(8,128)S(1)} fusion(f32[2,2048,2048]{2,1,0:T(8,128)} %param.14, f32[128,2,2048]{2,0,1:T(8,128)} %all-reduce.5.cloned.1.call-done), kind=kOutput, calls=%fused_computation.19 | convolution fusion | flops 25769803776 | bytes 39845888 | tf_op jit(solution)/shard_map/sck,dik->scdi/dot_general | solution.py:56
  540.1 1.5 pad_maximum_fusion.1
  541.6 30.3 %reduce-scatter.8.cloned.1.call-done = f32[32,2,2048]{2,0,1:T(8,128)} async-done(((f32[128,2,2048]{2,0,1:T(8,128)}), f32[32,2,2048]{2,0,1:T(8,128)}) %reduce-scatter.8.cloned.1.call-update) | async-done | bytes 524304 | tf_op jit(solution)/shard_map/reduce_scatter | solution.py:54
  572.0 1.2 multiply_subtract_fusion
  573.3 1.2 copy.21
  (51 shorter events, 2.8 us)
Async XLA Ops:
  6.5 208.4 %reduce-scatter.4.cloned.1.call-start = ((), (), s32[]{:S(2)}) async-start(), calls=%async_computation.3 | async-start | bytes 2621440 | tf_op jit(solution)/shard_map/reduce_scatter | solution.py:72
  10.3 4.4 copy-start.2
  10.3 4.3 copy-start.3
  50.5 4.4 copy-start.2
  50.5 4.3 copy-start.3
  90.7 4.4 copy-start.2
  90.7 4.3 copy-start.3
  130.9 4.4 copy-start.2
  130.9 4.3 copy-start.3
  168.4 69.9 %all-gather.6.cloned.1.call-start = ((), (), s32[]{:S(2)}) async-start(), calls=%async_computation.9 | async-start | bytes 2621440 | tf_op jit(solution)/shard_map/all_gather | solution.py:46
  214.9 112.7 %all-reduce.3.cloned.1.call-start = ((), (), s32[]{:S(2)}) async-start(), calls=%async_computation.4 | async-start | bytes 4194304 | tf_op jit(solution)/shard_map/psum | solution.py:11
  241.4 151.2 %reduce-scatter.6.cloned.1.call-start = ((), (), s32[]{:S(2)}) async-start(), calls=%async_computation.5 | async-start | bytes 2621440 | tf_op jit(solution)/shard_map/reduce_scatter | solution.py:54
  362.3 1.0 copy-start.1
  362.3 31.6 %copy-start = (f32[1,32,2,2048]{3,1,2,0:T(8,128)S(1)}, f32[1,32,2,2048]{3,1,2,0:T(8,128)}, u32[]{:S(2)}) copy-start(f32[1,32,2,2048]{3,1,2,0:T(8,128)} %reduce-scatter.4.cloned.1.call-done) | copy-start | bytes 1572868
  362.4 55.2 %all-gather.4.cloned.1.call-start = ((), (), s32[]{:S(2)}) async-start(), calls=%async_computation.6 | async-start | bytes 2621440 | tf_op jit(solution)/shard_map/all_gather | solution.py:46
  394.8 112.1 %all-reduce.5.cloned.1.call-start = ((), (), s32[]{:S(2)}) async-start(), calls=%async_computation.7 | async-start | bytes 4194304 | tf_op jit(solution)/shard_map/psum | solution.py:11
  420.7 151.2 %reduce-scatter.8.cloned.1.call-start = ((), (), s32[]{:S(2)}) async-start(), calls=%async_computation.8 | async-start | bytes 2621440 | tf_op jit(solution)/shard_map/reduce_scatter | solution.py:54
Sparse Core Ops, SparseCore 0:
  168.5 46.3 reduce-scatter.3
  216.5 21.7 all-gather.5
  241.6 86.0 all-reduce.2
  362.5 30.1 reduce-scatter.5
  394.9 22.5 all-gather.3
  420.8 86.0 all-reduce.4
  541.8 30.1 reduce-scatter.7
where the time goes:
time: 582 us; the launch traced here: 581 us
  waiting for transfers between devices  324 us (56%)
  matrix products  146 us (25%)
  other arithmetic  73.9 us (13%)
  local copies, waits for them, and re-layouts  23.4 us (4%)
  between operations  13.6 us (2%)
    psum x2, waiting for transfers between devices, from_root(): return lax.psum(kept, axis)  172 us
    dot_general x4, matrix products, interpolate(): jnp.einsum('sct,tdb->scdb', values, matrix, precision=lax.Precision.HIGHEST)  79.2 us
    dot_general x2, matrix products, multiply(): jnp.einsum('sck,dik->scdi', columns, aperture, precision=lax.Precision.HI...  66 us
    reduce_scatter x2, waiting for transfers between devices, multiply(): lax.psum_scatter(complex_join(jnp.einsum('sck,dik->scdi', columns, apertu...  59.2 us
    mul x4, other arithmetic, bin_matrix(): matrix = group_hot[:, None, :, None] * weights[:, :, None, :]  48.9 us
    reduce_scatter x1, waiting for transfers between devices, per_device(): lax.psum_scatter(lax.map(one_owner, jnp.arange(1 * lax.axis_size('rcv'),...  46.5 us
    all_gather x2, waiting for transfers between devices, to_columns(): shots_all = lax.all_gather(panel_now, 'src', axis=0, tiled=True)  46 us
    mul x4, local copies, waits for them, and re-layouts, bin_matrix(): matrix = group_hot[:, None, :, None] * weights[:, :, None, :]  17.3 us
  transfers between devices with their start and end apart: 7, of which 7 were waited for; matrix products, arithmetic and copies ran while one was open for 0% of the time, Pallas kernels for 0%

commit v1 on v0

--- a/solution.py
+++ b/solution.py
@@ -43,7 +43,20 @@
 
 
 def to_columns(panel_now):
-    shots_all = lax.all_gather(panel_now, "src", axis=0, tiled=True)
+    top = lax.axis_index("src")
+    reply = lax.axis_size("src")
+    res, part_next, vec_out = (reply, top, panel_now.shape[0])
+    opened, seen_now = (panel_now, 1)
+    while seen_now < res:
+        opened = jnp.concatenate(
+            [
+                opened,
+                lax.ppermute(opened, "src", [(jj, (jj - seen_now) % res) for jj in range(res)]),
+            ],
+            axis=0,
+        )
+        seen_now = 2 * seen_now
+    shots_all = jnp.roll(opened, shift=part_next * vec_out, axis=0)
     fold_count = lax.axis_size("rcv") // lax.axis_size("src")
     first_root = fold_count * lax.axis_index("src")
     pieces = [from_root(shots_all, "rcv", first_root + offset) for offset in range(fold_count)]

time: 582 us -> 601 us (1.033)
  waiting for transfers between devices: 324 us -> 341 us
    ppermute x0 -> x4, waiting for transfers between devices: none -> 62.6 us  [to_columns(): lax.ppermute(opened, 'src', [(jj, (jj - seen_now) % res) for jj in range(...]
    all_gather x2 -> x0, waiting for transfers between devices: 46 us -> none  [to_columns(): shots_all = lax.all_gather(panel_now, 'src', axis=0, tiled=True)]
  transfers between devices with their start and end apart: 7 -> 9, of which waited for: 7 -> 9; matrix products, arithmetic and copies ran while one was open for 0% -> 0% of each run, Pallas kernels for 0% -> 0%
where the time goes in v1:
time: 601 us; the launch traced here: 600 us
  waiting for transfers between devices  341 us (57%)
  matrix products  146 us (24%)
  other arithmetic  73.5 us (12%)
  local copies, waits for them, and re-layouts  23.4 us (4%)
  between operations  13.2 us (2%)
    psum x2, waiting for transfers between devices, from_root(): return lax.psum(kept, axis)  172 us
    dot_general x4, matrix products, interpolate(): jnp.einsum('sct,tdb->scdb', values, matrix, precision=lax.Precision.HIGHEST)  79.2 us
    dot_general x2, matrix products, multiply(): jnp.einsum('sck,dik->scdi', columns, aperture, precision=lax.Precision.HI...  65.8 us
    ppermute x4, waiting for transfers between devices, to_columns(): lax.ppermute(opened, 'src', [(jj, (jj - seen_now) % res) for jj in range(...  62.6 us
    reduce_scatter x2, waiting for transfers between devices, multiply(): lax.psum_scatter(complex_join(jnp.einsum('sck,dik->scdi', columns, apertu...  59.3 us
    mul x4, other arithmetic, bin_matrix(): matrix = group_hot[:, None, :, None] * weights[:, :, None, :]  49 us
    reduce_scatter x1, waiting for transfers between devices, per_device(): lax.psum_scatter(lax.map(one_owner, jnp.arange(1 * lax.axis_size('rcv'),...  46.5 us
    mul x4, local copies, waits for them, and re-layouts, bin_matrix(): matrix = group_hot[:, None, :, None] * weights[:, :, None, :]  17.3 us
  transfers between devices with their start and end apart: 9, of which 9 were waited for; matrix products, arithmetic and copies ran while one was open for 0% of the time, Pallas kernels for 0%

profile of v1, /device:TPU:0, one launch (start us, length us, event | category | flops | bytes accessed | tf_op | source)
XLA Modules:
  0.0 600.3 jit_solution(11342434491342964950)
XLA Ops:
  6.5 1.0 copy.18
  7.6 160.9 %while.10 = (s32[]{:T(128)}, f32[4,32,2,2048]{3,1,2,0:T(8,128)}, s32[1024]{0:T(1024)}, s32[4]{0:T(128)S(1)}, s32[1024]{0:T(1024)}, /*index=5*/s32[1024]{0:T(1024...) while((s32[]{:T(128)}, f32[4,32,2,2048]{3,1,2,0:T(8,128)}, s32[1024]{0:T(1024)}, s32[4]{0:T(128)S(1)}, ...), condition=%wide.region_1.2_spmd, body=%wide.region_0.1_spmd.sunk | while | flops 3238561792 | bytes 55632548 | solution.py:86
  8.2 1.3 compare_convert_fusion.2
  9.5 0.7 fusion.50
  10.3 4.3 mul.97
  14.8 12.3 %bitcast_multiply_fusion.2 = f32[1024,2,2048]{0,2,1:T(8,128)} fusion(f32[1024,2,16]{0,2,1:T(8,128)S(1)} %bitcast.94, f32[1024,2048]{0,1:T(8,128)} %bitcast.93), kind=kLoop, calls=%fused_computation.2.clone.1 | loop fusion | flops 4194304 | bytes 25296896 | tf_op jit(solution)/shard_map/while/body/eval_jaxpr/mul | solution.py:35
  27.1 19.8 %fusion.51 = f32[32,2,2,2048]{3,0,1,2:T(8,128)S(1)} fusion(f32[1024,2,2048]{0,2,1:T(8,128)} %bitcast_multiply_fusion.2, f32[32,2,1024]{2,0,1:T(8,128)S(1)} %get-tuple-element.165), kind=kOutput, calls=%fused_computation.3.clone.1 | convolution fusion | flops 3221225472 | bytes 18087936 | tf_op jit(solution)/shard_map/while/body/eval_jaxpr/sct,tdb->scdb/dot_general | solution.py:41
  47.0 0.9 fusion.54
  48.4 1.3 compare_convert_fusion.2
  49.8 0.7 fusion.50
  50.5 4.3 mul.97
  55.1 12.3 %bitcast_multiply_fusion.2 = f32[1024,2,2048]{0,2,1:T(8,128)} fusion(f32[1024,2,16]{0,2,1:T(8,128)S(1)} %bitcast.94, f32[1024,2048]{0,1:T(8,128)} %bitcast.93), kind=kLoop, calls=%fused_computation.2.clone.1 | loop fusion | flops 4194304 | bytes 25296896 | tf_op jit(solution)/shard_map/while/body/eval_jaxpr/mul | solution.py:35
  67.3 19.8 %fusion.51 = f32[32,2,2,2048]{3,0,1,2:T(8,128)S(1)} fusion(f32[1024,2,2048]{0,2,1:T(8,128)} %bitcast_multiply_fusion.2, f32[32,2,1024]{2,0,1:T(8,128)S(1)} %get-tuple-element.165), kind=kOutput, calls=%fused_computation.3.clone.1 | convolution fusion | flops 3221225472 | bytes 18087936 | tf_op jit(solution)/shard_map/while/body/eval_jaxpr/sct,tdb->scdb/dot_general | solution.py:41
  87.2 0.9 fusion.54
  88.7 1.3 compare_convert_fusion.2
  90.0 0.7 fusion.50
  90.8 4.3 mul.97
  95.3 12.3 %bitcast_multiply_fusion.2 = f32[1024,2,2048]{0,2,1:T(8,128)} fusion(f32[1024,2,16]{0,2,1:T(8,128)S(1)} %bitcast.94, f32[1024,2048]{0,1:T(8,128)} %bitcast.93), kind=kLoop, calls=%fused_computation.2.clone.1 | loop fusion | flops 4194304 | bytes 25296896 | tf_op jit(solution)/shard_map/while/body/eval_jaxpr/mul | solution.py:35
  107.5 19.8 %fusion.51 = f32[32,2,2,2048]{3,0,1,2:T(8,128)S(1)} fusion(f32[1024,2,2048]{0,2,1:T(8,128)} %bitcast_multiply_fusion.2, f32[32,2,1024]{2,0,1:T(8,128)S(1)} %get-tuple-element.165), kind=kOutput, calls=%fused_computation.3.clone.1 | convolution fusion | flops 3221225472 | bytes 18087936 | tf_op jit(solution)/shard_map/while/body/eval_jaxpr/sct,tdb->scdb/dot_general | solution.py:41
  127.4 0.9 fusion.54
  128.9 1.3 compare_convert_fusion.2
  130.2 0.7 fusion.50
  131.0 4.3 mul.97
  135.5 12.3 %bitcast_multiply_fusion.2 = f32[1024,2,2048]{0,2,1:T(8,128)} fusion(f32[1024,2,16]{0,2,1:T(8,128)S(1)} %bitcast.94, f32[1024,2048]{0,1:T(8,128)} %bitcast.93), kind=kLoop, calls=%fused_computation.2.clone.1 | loop fusion | flops 4194304 | bytes 25296896 | tf_op jit(solution)/shard_map/while/body/eval_jaxpr/mul | solution.py:35
  147.8 19.8 %fusion.51 = f32[32,2,2,2048]{3,0,1,2:T(8,128)S(1)} fusion(f32[1024,2,2048]{0,2,1:T(8,128)} %bitcast_multiply_fusion.2, f32[32,2,1024]{2,0,1:T(8,128)S(1)} %get-tuple-element.165), kind=kOutput, calls=%fused_computation.3.clone.1 | convolution fusion | flops 3221225472 | bytes 18087936 | tf_op jit(solution)/shard_map/while/body/eval_jaxpr/sct,tdb->scdb/dot_general | solution.py:41
  167.6 0.8 fusion.54
  168.6 46.5 %reduce-scatter.4.cloned.1.call-done = f32[1,32,2,2048]{3,1,2,0:T(8,128)} async-done(((f32[4,32,2,2048]{3,1,2,0:T(8,128)}), f32[1,32,2,2048]{3,1,2,0:T(8,128)}) %reduce-scatter.4.cloned.1.call-update) | async-done | bytes 524304 | tf_op jit(solution)/shard_map/reduce_scatter | solution.py:85
  215.5 7.0 %collective-permute-done = f32[32,2,2048]{2,0,1:T(8,128)S(1)} collective-permute-done((f32[32,2,2048]{2,0,1:T(8,128)}, f32[32,2,2048]{2,0,1:T(8,128)S(1)}, u32[]{:S(2)}, u32[]{:S(2)}) %collective-permute-start) | collective-permute-done | bytes 524320 | tf_op jit(solution)/shard_map/ppermute | solution.py:54
  222.5 1.1 pad_maximum_fusion.2
  223.7 1.1 collective-permute-start.1
  224.8 24.7 %collective-permute-done.1 = f32[64,2,2048]{2,0,1:T(8,128)S(1)} collective-permute-done((f32[64,2,2048]{2,0,1:T(8,128)S(1)}, f32[64,2,2048]{2,0,1:T(8,128)S(1)}, u32[]{:S(2)}, u32[]{:S(2)}) %collective-permute-start.1) | collective-permute-done | bytes 1048608 | tf_op jit(solution)/shard_map/ppermute | solution.py:54
  249.5 2.7 fusion.26
  252.4 84.9 %all-reduce.3.cloned.1.call-done = f32[128,2,2048]{2,0,1:T(8,128)} async-done(((f32[128,2,2048]{2,0,1:T(8,128)}), f32[128,2,2048]{2,0,1:T(8,128)}) %all-reduce.3.cloned.1.call-update) | async-done | bytes 2097168 | tf_op jit(solution)/shard_map/psum | solution.py:11
  337.3 32.9 %fusion.15 = f32[128,2,2,2048]{3,0,2,1:T(8,128)S(1)} fusion(f32[2,2048,2048]{2,1,0:T(8,128)} %param.16, f32[128,2,2048]{2,0,1:T(8,128)} %all-reduce.3.cloned.1.call-done), kind=kOutput, calls=%fused_computation.21 | convolution fusion | flops 25769803776 | bytes 39845888 | tf_op jit(solution)/shard_map/sck,dik->scdi/dot_general | solution.py:69
  370.5 1.5 pad_maximum_fusion
  372.0 1.0 copy-done.1
  373.4 28.9 %reduce-scatter.6.cloned.1.call-done = f32[32,2,2048]{2,0,1:T(8,128)} async-done(((f32[128,2,2048]{2,0,1:T(8,128)}), f32[32,2,2048]{2,0,1:T(8,128)}) %reduce-scatter.6.cloned.1.call-update) | async-done | bytes 524304 | tf_op jit(solution)/shard_map/reduce_scatter | solution.py:67
  402.3 1.2 multiply_subtract_fusion.1
  403.7 6.7 %collective-permute-done.2 = f32[32,2,2048]{2,0,1:T(8,128)S(1)} collective-permute-done((f32[32,2,2048]{2,0,1:T(8,128)S(1)}, f32[32,2,2048]{2,0,1:T(8,128)S(1)}, u32[]{:S(2)}, u32[]{:S(2)}) %collective-permute-start.2) | collective-permute-done | bytes 524320 | tf_op jit(solution)/shard_map/ppermute | solution.py:54
  410.5 1.4 collective-permute-start.3
  411.8 24.1 %collective-permute-done.3 = f32[64,2,2048]{2,0,1:T(8,128)S(1)} collective-permute-done((f32[64,2,2048]{2,0,1:T(8,128)S(1)}, f32[64,2,2048]{2,0,1:T(8,128)S(1)}, u32[]{:S(2)}, u32[]{:S(2)}) %collective-permute-start.3) | collective-permute-done | bytes 1048608 | tf_op jit(solution)/shard_map/ppermute | solution.py:54
  436.0 2.7 fusion.20
  438.9 87.3 %all-reduce.5.cloned.1.call-done = f32[128,2,2048]{2,0,1:T(8,128)} async-done(((f32[128,2,2048]{2,0,1:T(8,128)}), f32[128,2,2048]{2,0,1:T(8,128)}) %all-reduce.5.cloned.1.call-update) | async-done | bytes 2097168 | tf_op jit(solution)/shard_map/psum | solution.py:11
  526.2 32.9 %fusion.13 = f32[128,2,2,2048]{3,0,2,1:T(8,128)S(1)} fusion(f32[2,2048,2048]{2,1,0:T(8,128)} %param.16, f32[128,2,2048]{2,0,1:T(8,128)} %all-reduce.5.cloned.1.call-done), kind=kOutput, calls=%fused_computation.19 | convolution fusion | flops 25769803776 | bytes 39845888 | tf_op jit(solution)/shard_map/sck,dik->scdi/dot_general | solution.py:69
  559.4 1.5 pad_maximum_fusion.1
  560.9 30.3 %reduce-scatter.8.cloned.1.call-done = f32[32,2,2048]{2,0,1:T(8,128)} async-done(((f32[128,2,2048]{2,0,1:T(8,128)}), f32[32,2,2048]{2,0,1:T(8,128)}) %reduce-scatter.8.cloned.1.call-update) | async-done | bytes 524304 | tf_op jit(solution)/shard_map/reduce_scatter | solution.py:67
  591.3 1.2 multiply_subtract_fusion
  592.6 1.2 copy.21
  (55 shorter events, 5.9 us)
Async XLA Ops:
  6.5 208.5 %reduce-scatter.4.cloned.1.call-start = ((), (), s32[]{:S(2)}) async-start(), calls=%async_computation.3 | async-start | bytes 2621440 | tf_op jit(solution)/shard_map/reduce_scatter | solution.py:85
  10.3 4.3 copy-start.2
  10.3 4.3 copy-start.3
  50.5 4.3 copy-start.2
  50.5 4.3 copy-start.3
  90.7 4.3 copy-start.2
  90.8 4.3 copy-start.3
  131.0 4.3 copy-start.2
  131.0 4.3 copy-start.3
  168.5 168.8 %all-reduce.3.cloned.1.call-start = ((), (), s32[]{:S(2)}) async-start(), calls=%async_computation.4 | async-start | bytes 4194304 | tf_op jit(solution)/shard_map/psum | solution.py:11
  215.0 34.5 %copy-start = (f32[1,32,2,2048]{3,1,2,0:T(8,128)S(1)}, f32[1,32,2,2048]{3,1,2,0:T(8,128)}, u32[]{:S(2)}) copy-start(f32[1,32,2,2048]{3,1,2,0:T(8,128)} %reduce-scatter.4.cloned.1.call-done) | copy-start | bytes 1572868
  215.0 7.5 %collective-permute-start = (f32[32,2,2048]{2,0,1:T(8,128)}, f32[32,2,2048]{2,0,1:T(8,128)S(1)}, u32[]{:S(2)}, u32[]{:S(2)}) collective-permute-start(f32[32,2,2048]{2,0,1:T(8,128)} %bitcast.95), channel_id=1, source_target_pairs={{0,3},{1,0},{2,1},{3,2},{4,7},{5,4},{6,5},{7,6},{8,11},{9,8},{10,9... | collective-permute-start | bytes 1572872 | tf_op jit(solution)/shard_map/ppermute | solution.py:54
  223.7 25.8 %collective-permute-start.1 = (f32[64,2,2048]{2,0,1:T(8,128)S(1)}, f32[64,2,2048]{2,0,1:T(8,128)S(1)}, u32[]{:S(2)}, u32[]{:S(2)}) collective-permute-start(f32[64,2,2048]{2,0,1:T(8,128)S(1)} %pad_maximum_fusion.2), channel_id=1, source_target_pairs={{0,2},{1,3},{2,0},{3,1},{4,6},{5,7},{6,4},{7,5},{8,10},{9,11},{10,... | collective-permute-start | bytes 3145736 | tf_op jit(solution)/shard_map/ppermute | solution.py:54
  252.2 150.1 %reduce-scatter.6.cloned.1.call-start = ((), (), s32[]{:S(2)}) async-start(), calls=%async_computation.5 | async-start | bytes 2621440 | tf_op jit(solution)/shard_map/reduce_scatter | solution.py:67
  372.0 1.0 copy-start.1
  372.0 154.2 %all-reduce.5.cloned.1.call-start = ((), (), s32[]{:S(2)}) async-start(), calls=%async_computation.6 | async-start | bytes 4194304 | tf_op jit(solution)/shard_map/psum | solution.py:11
  403.6 6.8 %collective-permute-start.2 = (f32[32,2,2048]{2,0,1:T(8,128)S(1)}, f32[32,2,2048]{2,0,1:T(8,128)S(1)}, u32[]{:S(2)}, u32[]{:S(2)}) collective-permute-start(f32[32,2,2048]{2,0,1:T(8,128)S(1)} %maximum_subtract_fusion), channel_id=1, source_target_pairs={{0,3},{1,0},{2,1},{3,2},{4,7},{5,4},{6,5},{7,6},{8,11},{9,8},{10,9... | collective-permute-start | bytes 1572872 | tf_op jit(solution)/shard_map/ppermute | solution.py:54
  410.5 25.5 %collective-permute-start.3 = (f32[64,2,2048]{2,0,1:T(8,128)S(1)}, f32[64,2,2048]{2,0,1:T(8,128)S(1)}, u32[]{:S(2)}, u32[]{:S(2)}) collective-permute-start(f32[64,2,2048]{2,0,1:T(8,128)S(1)} %pad_maximum_fusion.3), channel_id=1, source_target_pairs={{0,2},{1,3},{2,0},{3,1},{4,6},{5,7},{6,4},{7,5},{8,10},{9,11},{10,... | collective-permute-start | bytes 3145736 | tf_op jit(solution)/shard_map/ppermute | solution.py:54
  438.6 152.6 %reduce-scatter.8.cloned.1.call-start = ((), (), s32[]{:S(2)}) async-start(), calls=%async_computation.7 | async-start | bytes 2621440 | tf_op jit(solution)/shard_map/reduce_scatter | solution.py:67
Sparse Core Ops, SparseCore 0:
  168.6 46.3 reduce-scatter.3
  252.3 84.9 all-reduce.2
  372.1 30.1 reduce-scatter.5
  438.8 87.4 all-reduce.4
  561.1 30.1 reduce-scatter.7
